TPU v7x, 128 devices: a whole 4x4x4 slice. The times are simulated.
128 devices in a mesh: bx: 16 (over z, x), by: 8 (over y, core).
Axes of the slice: x: 4, y: 4, z: 4, core: 2. Of those that a mesh axis runs over, the one named last changes fastest.
Arguments:
- brick_ids: int32 [16384, 3], P(('bx', 'by')), may hold values from 0 to 255, all different within a row; in each aligned block of 128 rows (0 to 127, 128 to 255, ...) at most 5 rows name the same one
- cell_index: int32 [6, 3, 3, 16384], P(None, None, None, ('bx', 'by')), may hold values from 0 to 14
- cell_frac: float32 [6, 3, 3, 16384], P(None, None, None, ('bx', 'by')), may hold values from 0 to 1
- step_length: float32 [3, 3, 16384], P(None, None, ('bx', 'by')), may hold values from 0.01 to 0.05
- target: float32 [3, 16384], P(None, ('bx', 'by')), may hold values from 0 to 1
- planes: bfloat16 [256, 3, 256, 128], P(('bx', 'by')), may hold values from -6 to 6
- first_layer: bfloat16 [256, 128, 256], P(('bx', 'by')), may hold values from -0.5 to 0.5
- last_layer: bfloat16 [256, 4, 256], P(('bx', 'by')), may hold values from -0.375 to 0.375
Outputs:
- colour: float32 [3, 16384], P(None, ('bx', 'by'))
- plane_grad: float32 [256, 3, 256, 128], P(('bx', 'by'))
- first_grad: float32 [256, 128, 256], P(('bx', 'by'))
- last_grad: float32 [256, 4, 256], P(('bx', 'by'))
Inputs may be any that keep to these rules, and one draw needn't show every extreme that they name: `brick_ids`: row r lists the 3 different bricks that ray r crosses, in the order in which it crosses them; among the rays of one device no brick is named more than 5 times.
All inputs are finite; a program needn't handle non-finite values.
Results may differ from a plain program's by a relative error of at most 0.007.
The roundings to bfloat16 on the way count: a program that leaves them out, or rounds other values in their place, can miss the bound.
Values sent between devices are 32-bit elements; how exact they have to be, the bound alone decides.
No kernel may reach another device: no remote copies, remote signals or barrier semaphores. Data moves between devices by JAX's collectives and lax.ppermute only.
A program may use at most 64 MiB of HBM per device.

v0:
```python
import math

import jax
import jax.numpy as jnp
from jax import lax
from jax.experimental import pallas as pl
from jax.experimental.pallas import tpu as pltpu
from jax.sharding import PartitionSpec as P

F32 = jnp.float32
BF16 = jnp.bfloat16
AXES = ("bx", "by")


def pieces_of(value):
    high = value.astype(BF16)
    rest = value - high.astype(F32)
    middle = rest.astype(BF16)
    low = (rest - middle.astype(F32)).astype(BF16)
    return high, middle, low


def dot_t(a, b):
    return lax.dot_general(a, b, (((1,), (1,)), ((), ())), preferred_element_type=F32)


def row_iota(shape):
    return lax.broadcasted_iota(jnp.int32, shape, 0)


def scatter_kernel(ids_ref, cell_ref, frac_ref, out_ref, route_ref, coord_ref, *, lb, cap, devices):
    crossed, rays = ids_ref.shape
    fields, _, samples, _ = cell_ref.shape
    bricks = lb * devices
    ids = [ids_ref[c : c + 1, :] for c in range(crossed)]
    brick_rows = row_iota((bricks, rays))
    member = [brick_rows == jnp.broadcast_to(i, (bricks, rays)) for i in ids]
    named = member[0].astype(F32)
    for c in range(1, crossed):
        named = named + member[c].astype(F32)
    earlier = row_iota((rays, rays)) < lax.broadcasted_iota(jnp.int32, (rays, rays), 1)
    before = jnp.dot(
        named.astype(BF16), earlier.astype(F32).astype(BF16), preferred_element_type=F32
    )
    coord_ref[...] = jnp.zeros(coord_ref.shape, F32)
    shift = lb.bit_length() - 1
    device_rows = row_iota((devices, rays))
    hots, slots = [], [[], [], []]
    span = fields * 4
    pad = out_ref.shape[1] - lb * cap * span
    for c in range(crossed):
        rank = jnp.sum(jnp.where(member[c], before, 0.0), axis=0, keepdims=True).astype(jnp.int32)
        device = lax.shift_right_logical(ids[c], shift)
        slot = (ids[c] & (lb - 1)) * cap + rank
        route_ref[c : c + 1, :] = device
        route_ref[4 + c : 5 + c, :] = slot
        hots.append((device_rows == jnp.broadcast_to(device, (devices, rays))).astype(F32).astype(BF16))
        for f in range(fields):
            coord_ref[c, f * 4 : f * 4 + samples, :] = cell_ref[f, c].astype(F32) + frac_ref[f, c]
        value = coord_ref[c]
        here = jnp.broadcast_to(slot, (span, rays))
        rows = [jnp.where(here == q, value, 0.0) for q in range(lb * cap)]
        if pad:
            rows.append(jnp.zeros((pad, rays), F32))
        for n, part in enumerate(pieces_of(jnp.concatenate(rows, axis=0))):
            slots[n].append(part)
    hot = jnp.concatenate(hots, axis=1)
    total = None
    for n in range(3):
        part = dot_t(hot, jnp.concatenate(slots[n], axis=1))
        total = part if total is None else total + part
    out_ref[...] = total


def hat(value, place):
    return jnp.maximum(0.0, 1.0 - jnp.abs(value - place))


def result_row(q, s, lb, cap):
    return q * 8 + s * 4 if s < 2 else lb * cap * 8 + q * 4


def forward_kernel(
    arrived_ref, planes_ref, first_ref, last_ref, out_ref, table_ref, feature_ref, hidden_ref,
    slope_ref, turned_ref, rows_ref, result_ref, *, lb, cap, samples
):
    cells = planes_ref.shape[2]
    side = math.isqrt(cells)
    lanes = arrived_ref.shape[0]
    brick = pl.program_id(0)
    span = 24
    orients = planes_ref.shape[1]

    @pl.when(brick == 0)
    def _():
        turned_ref[...] = arrived_ref[...].T
        result_ref[...] = jnp.zeros(result_ref.shape, F32)

    rows_ref[...] = turned_ref[pl.ds(pl.multiple_of(brick * (cap * span), 8), cap * span), :]
    place = row_iota((side, lanes)).astype(F32)
    for k in range(cap):
        for s in range(samples):
            block = (k * samples + s) * lanes
            for p in range(orients):
                at = k * span + 8 * p + s
                x = jnp.broadcast_to(rows_ref[at : at + 1, :], (side, lanes))
                y = jnp.broadcast_to(rows_ref[at + 4 : at + 5, :], (side, lanes))
                across = hat(y, place)
                for a in range(side):
                    table_ref[0, p * cells + a * side : p * cells + (a + 1) * side, block : block + lanes] = (
                        hat(x, float(a)) * across
                    ).astype(BF16)
    planes_t = planes_ref[0].reshape(orients * cells, -1).T
    feature = jnp.dot(planes_t, table_ref[0], preferred_element_type=F32).astype(BF16)
    feature_ref[0] = feature
    before = jnp.dot(first_ref[0].T, feature, preferred_element_type=F32)
    hidden = jnp.maximum(before, 0.0).astype(BF16)
    hidden_ref[0] = hidden
    raw = jnp.dot(last_ref[0], hidden, preferred_element_type=F32)
    gate = jax.nn.sigmoid(raw)
    is_density = row_iota(raw.shape) == 0
    result = jnp.where(is_density, jax.nn.softplus(raw), gate)
    slope_ref[0] = jnp.where(is_density, gate, gate * (1.0 - gate))
    for b in range(lb):

        @pl.when(brick == b)
        def _(b=b):
            for k in range(cap):
                for s in range(samples):
                    block = (k * samples + s) * lanes
                    row = result_row(b * cap + k, s, lb, cap)
                    result_ref[row : row + 4, :] = result[:, block : block + lanes]

    @pl.when(brick == lb - 1)
    def _():
        out_ref[...] = result_ref[...].T


def render_kernel(
    returned_ref, route_ref, step_ref, target_ref, colour_ref, out_ref, *, lb, cap
):
    devices = returned_ref.shape[0]
    crossed, samples, rays = step_ref.shape
    slots = lb * cap
    turned = returned_ref[...].T
    parts = pieces_of(turned)
    device_rows = row_iota((devices, rays))
    hots = [
        (device_rows == jnp.broadcast_to(route_ref[c : c + 1, :], (devices, rays))).astype(F32).astype(BF16)
        for c in range(crossed)
    ]
    hot = jnp.concatenate(hots, axis=1)
    fetched = None
    for part in parts:
        piece = jnp.dot(part, hot, preferred_element_type=F32)
        fetched = piece if fetched is None else fetched + piece
    parity = lax.shift_right_logical(row_iota((8, rays)), 2)
    picked = []
    for c in range(crossed):
        slot = jnp.broadcast_to(route_ref[4 + c : 5 + c, :], (8, rays))
        block = fetched[:, c * rays : (c + 1) * rays]
        two = jnp.zeros((8, rays), F32)
        for q in range(slots):
            two = two + jnp.where(slot == q, block[q * 8 : q * 8 + 8], 0.0)
        third = jnp.zeros((8, rays), F32)
        for h in range(slots // 2):
            at = slots * 8 + h * 8
            held = slot == parity + 2 * h
            third = third + jnp.where(held, block[at : at + 8], 0.0)
        third = third[0:4] + third[4:8]
        picked += [two[0:4], two[4:8], third]
    steps = [step_ref[c, s : s + 1, :] for c in range(crossed) for s in range(samples)]
    count = crossed * samples
    depth = [picked[i][0:1] * steps[i] for i in range(count)]
    inclusive, running = [], None
    for i in range(count):
        running = depth[i] if running is None else running + depth[i]
        inclusive.append(running)
    weight = []
    for i in range(count):
        through = 1.0 - jnp.exp(-depth[i])
        weight.append(through if i == 0 else jnp.exp(-inclusive[i - 1]) * through)
    colour = None
    for i in range(count):
        term = weight[i] * picked[i][1:4]
        colour = term if colour is None else colour + term
    colour_ref[...] = colour
    residual = colour - target_ref[...]
    dots = [jnp.sum(picked[i][1:4] * residual, axis=0, keepdims=True) for i in range(count)]
    after = [None] * count
    tail = jnp.zeros((1, rays), F32)
    for i in reversed(range(count)):
        after[i] = tail
        tail = tail + weight[i] * dots[i]
    cots = []
    for i in range(count):
        density_cot = (jnp.exp(-inclusive[i]) * dots[i] - after[i]) * steps[i]
        cots.append(jnp.concatenate([density_cot, weight[i] * residual], axis=0))
    placed = [[], [], []]
    for c in range(crossed):
        slot = jnp.broadcast_to(route_ref[4 + c : 5 + c, :], (8, rays))
        two = jnp.concatenate([cots[c * samples], cots[c * samples + 1]], axis=0)
        third = jnp.concatenate([cots[c * samples + 2]] * 2, axis=0)
        rows = [jnp.where(slot == q, two, 0.0) for q in range(slots)]
        for h in range(slots // 2):
            rows.append(jnp.where(slot == parity + 2 * h, third, 0.0))
        pad = out_ref.shape[1] - slots * 12
        if pad:
            rows.append(jnp.zeros((pad, rays), F32))
        for n, part in enumerate(pieces_of(jnp.concatenate(rows, axis=0))):
            placed[n].append(part)
    total = None
    for n in range(3):
        part = dot_t(hot, jnp.concatenate(placed[n], axis=1))
        total = part if total is None else total + part
    out_ref[...] = total


def backward_kernel(
    arrived_ref, table_ref, feature_ref, hidden_ref, slope_ref, first_ref, last_ref,
    plane_ref, first_grad_ref, last_grad_ref, turned_ref, cot_ref, *, lb, cap, samples
):
    lanes = arrived_ref.shape[0]
    brick = pl.program_id(0)

    @pl.when(brick == 0)
    def _():
        turned_ref[...] = arrived_ref[...].T

    for b in range(lb):

        @pl.when(brick == b)
        def _(b=b):
            for k in range(cap):
                for s in range(samples):
                    block = (k * samples + s) * lanes
                    row = result_row(b * cap + k, s, lb, cap)
                    cot_ref[:, block : block + lanes] = turned_ref[row : row + 4, :]

    raw_cot = (cot_ref[...] * slope_ref[0]).astype(BF16)
    hidden = hidden_ref[0]
    last_grad_ref[0] = dot_t(raw_cot, hidden)
    hidden_cot = jnp.dot(last_ref[0].astype(F32).T.astype(BF16), raw_cot, preferred_element_type=F32)
    before_cot = jnp.where(hidden.astype(F32) > 0, hidden_cot, 0.0).astype(BF16)
    first_grad_ref[0] = dot_t(feature_ref[0], before_cot)
    feature_cot = jnp.dot(first_ref[0], before_cot, preferred_element_type=F32).astype(BF16)
    orients, cells, channels = plane_ref.shape[1:]
    plane_ref[0] = dot_t(table_ref[0], feature_cot).reshape(orients, cells, channels)


def exchange(block):
    return lax.all_to_all(block, AXES, split_axis=0, concat_axis=0, tiled=True)


def whole(shape):
    return pl.BlockSpec(shape, lambda *_: (0,) * len(shape))


def per_brick(shape):
    return pl.BlockSpec((1,) + tuple(shape[1:]), lambda b: (b,) + (0,) * (len(shape) - 1))


def on_device(
    brick_ids, cell_index, cell_frac, step_length, target, planes, first_layer, last_layer
):
    devices = lax.axis_size("bx") * lax.axis_size("by")
    lb, orients, cells, channels = planes.shape
    rays, crossed = brick_ids.shape
    samples = step_length.shape[1]
    hidden_units = first_layer.shape[2]
    bricks = lb * devices
    cap = max(2, (3 * rays * crossed + bricks - 1) // bricks)
    fields = cell_index.shape[0]
    width = -(-lb * cap * fields * 4 // 128) * 128
    back = -(-lb * cap * 12 // 128) * 128
    rows = cap * samples * devices
    shape = jax.ShapeDtypeStruct

    outgoing, route = pl.pallas_call(
        lambda *refs: scatter_kernel(*refs, lb=lb, cap=cap, devices=devices),
        out_shape=(shape((devices, width), F32), shape((8, rays), jnp.int32)),
        scratch_shapes=[pltpu.VMEM((crossed, fields * 4, rays), F32)],
        name="scatter",
    )(brick_ids.T, cell_index, cell_frac)
    arrived = exchange(outgoing)

    saved = (
        shape((lb, orients * cells, rows), BF16),
        shape((lb, channels, rows), BF16),
        shape((lb, hidden_units, rows), BF16),
        shape((lb, 4, rows), F32),
    )
    results, table, feature, hidden, slope = pl.pallas_call(
        lambda *refs: forward_kernel(*refs, lb=lb, cap=cap, samples=samples),
        grid=(lb,),
        in_specs=[
            whole(arrived.shape), per_brick(planes.shape), per_brick(first_layer.shape),
            per_brick(last_layer.shape),
        ],
        out_specs=(whole((devices, back)),) + tuple(per_brick(s.shape) for s in saved),
        out_shape=(shape((devices, back), F32),) + saved,
        scratch_shapes=[
            pltpu.VMEM((width, devices), F32),
            pltpu.VMEM((cap * fields * 4, devices), F32),
            pltpu.VMEM((back, devices), F32),
        ],
        name="forward",
    )(arrived, planes, first_layer, last_layer)
    returned = exchange(results)

    colour, cot_out = pl.pallas_call(
        lambda *refs: render_kernel(*refs, lb=lb, cap=cap),
        out_shape=(shape(target.shape, F32), shape((devices, back), F32)),
        name="render",
    )(returned, route, step_length, target)
    cot_in = exchange(cot_out)

    grads = (
        shape(planes.shape, F32),
        shape(first_layer.shape, F32),
        shape(last_layer.shape, F32),
    )
    plane_grad, first_grad, last_grad = pl.pallas_call(
        lambda *refs: backward_kernel(*refs, lb=lb, cap=cap, samples=samples),
        grid=(lb,),
        in_specs=[whole(cot_in.shape)] + [per_brick(s.shape) for s in saved]
        + [per_brick(first_layer.shape), per_brick(last_layer.shape)],
        out_specs=tuple(per_brick(s.shape) for s in grads),
        out_shape=grads,
        scratch_shapes=[pltpu.VMEM((back, devices), F32), pltpu.VMEM((4, rows), F32)],
        name="backward",
    )(cot_in, table, feature, hidden, slope, first_layer, last_layer)
    return colour, plane_grad, first_grad, last_grad


def solution(mesh):
    return jax.shard_map(
        on_device,
        mesh=mesh,
        in_specs=(
            P(AXES, None),
            P(None, None, None, AXES),
            P(None, None, None, AXES),
            P(None, None, AXES),
            P(None, AXES),
            P(AXES, None, None, None),
            P(AXES, None, None),
            P(AXES, None, None),
        ),
        out_specs=(
            P(None, AXES),
            P(AXES, None, None, None),
            P(AXES, None, None),
            P(AXES, None, None),
        ),
        check_vma=False,
    )
```

profile of v0, /device:TPU:1, one launch (start us, length us, event | category | flops | bytes accessed | tf_op | source)
XLA Modules:
  0.0 72.4 jit_solution(17996892085228893900)
XLA Ops:
  0.6 2.0 %scatter.1 = (f32[128,256]{1,0:T(8,128)}, s32[8,128]{1,0:T(8,128)}) custom-call(s32[3,128]{1,0:T(4,128)} %bitcast.19, s32[6,3,3,128]{3,2,1,0:T(4,128)} %refs_1_.2, f32[6,3,3,128]{3,2,1,0:T(4,128)} %refs_2_.3), custom_call_target="tpu_custom_call" | custom-call | tf_op jit(solution)/shard_map/scatter/pallas_call | solution.py:279
  2.6 1.0 %copy.12 = f32[128,1,256]{2,1,0:T(1,128)S(1)} copy(f32[128,1,256]{2,0,1:T(8,128)} %bitcast.16) | data formatting | bytes 262144 | tf_op jit(solution)/shard_map/all_to_all | solution.py:252
  3.7 21.4 %all_to_all.33 = f32[128,1,256]{2,1,0:T(1,128)S(1)} all-to-all(f32[128,1,256]{2,1,0:T(1,128)S(1)} %copy.12), channel_id=1, replica_groups=mesh['bx'=16,'by'=8] {'bx','by'}, dimensions={0} | all-to-all | bytes 262144 | tf_op jit(solution)/shard_map/all_to_all | solution.py:252
  25.1 0.7 copy.17
  25.8 7.4 %forward.1 = (f32[128,128]{1,0:T(8,128)}, bf16[2,768,1920]{2,1,0:T(8,128)(2,1)}, bf16[2,128,1920]{2,1,0:T(8,128)(2,1)}, bf16[2,256,1920]{2,1,0:T(8,128)(2,1)}, f32[2,4,1920]{2,1,0:T(4,128)}) custom-call(f32[128,256]{1,0:T(8,128)} %bitcast.13, bf16[2,3,256,128]{3,2,1,0:T(8,128)(2,1)} %refs_1_.3, bf16[2,128,256]{2,1,0:T(8,128)(2,1)} %refs_5_.1, ...), custom_call_target="tpu_custom_call" | custom-call | tf_op jit(solution)/shard_map/forward/pallas_call | solution.py:293
  33.2 14.7 %all_to_all.34 = f32[128,1,128]{2,1,0:T(1,128)} all-to-all(f32[128,1,128]{2,1,0:T(1,128)} %bitcast.17), channel_id=1, replica_groups=mesh['bx'=16,'by'=8] {'bx','by'}, dimensions={0} | all-to-all | bytes 131072 | tf_op jit(solution)/shard_map/all_to_all | solution.py:252
  47.9 2.1 %render.1 = (f32[3,128]{1,0:T(4,128)}, f32[128,128]{1,0:T(8,128)}) custom-call(f32[128,128]{1,0:T(8,128)} %bitcast.15, s32[8,128]{1,0:T(8,128)} %get-tuple-element.18.refs_1_, f32[3,3,128]{2,1,0:T(4,128)} %refs_2_.5, f32[3,128]{1,0:T(4,128)} %refs_3_.3), custom_call_target="tpu_custom_call" | custom-call | tf_op jit(solution)/shard_map/render/pallas_call | solution.py:311
  50.1 15.2 %all_to_all.35 = f32[128,1,128]{2,1,0:T(1,128)} all-to-all(f32[128,1,128]{2,1,0:T(1,128)} %bitcast.18), channel_id=1, replica_groups=mesh['bx'=16,'by'=8] {'bx','by'}, dimensions={0} | all-to-all | bytes 131072 | tf_op jit(solution)/shard_map/all_to_all | solution.py:252
  65.2 7.2 %backward.1 = (f32[2,3,256,128]{3,2,1,0:T(8,128)}, f32[2,128,256]{2,1,0:T(8,128)}, f32[2,4,256]{2,1,0:T(4,128)}) custom-call(f32[128,128]{1,0:T(8,128)} %bitcast.14, bf16[2,768,1920]{2,1,0:T(8,128)(2,1)} %get-tuple-element.21.refs_1_, bf16[2,128,1920]{2,1,0:T(8,128)(2,1)} %get-tuple-element.22.refs_2_, bf16[2,256,1920]{2,1,0:T(8,128)(2,1)} %get-tuple-element.23.refs_3_, ...), custom_call_target="tpu_custom_call" | custom-call | tf_op jit(solution)/shard_map/backward/pallas_call | solution.py:323
where the time goes:
time: 72.8 us; the launch traced here: 72.4 us
  blocking collectives  51.3 us (70%)
  Pallas kernels  18.8 us (26%)
  local copies, waits for them, and re-layouts  1.7 us (2%)
    all_to_all x3, blocking collectives, exchange(): return lax.all_to_all(block, AXES, split_axis=0, concat_axis=0, tiled=True)  51.3 us
    pallas_call x1, Pallas kernels, on_device(): pl.pallas_call(lambda *refs: forward_kernel(*refs, lb=lb, cap=cap, sample...  7.44 us
    pallas_call x1, Pallas kernels, on_device(): pl.pallas_call(lambda *refs: backward_kernel(*refs, lb=lb, cap=cap, sampl...  7.22 us
    pallas_call x1, Pallas kernels, on_device(): pl.pallas_call(lambda *refs: render_kernel(*refs, lb=lb, cap=cap), out_sh...  2.14 us
    pallas_call x1, Pallas kernels, on_device(): pl.pallas_call(lambda *refs: scatter_kernel(*refs, lb=lb, cap=cap, device...  2 us

commit v1 on v0

--- a/solution.py
+++ b/solution.py
@@ -28,7 +28,20 @@
     return lax.broadcasted_iota(jnp.int32, shape, 0)
 
 
-def scatter_kernel(ids_ref, cell_ref, frac_ref, out_ref, route_ref, coord_ref, *, lb, cap, devices):
+def scatter_kernel(
+    ids_in, cell_in, frac_in, *refs, lb, cap, devices
+):
+    carried = len(refs) // 2 - 3
+    moved_in, (out_ref, route_ref), moved_out = refs[:carried], refs[carried : carried + 2], refs[carried + 2 : 2 * carried + 2]
+    ids_ref, cell_ref, frac_ref, coord_ref, sems = refs[2 * carried + 2 :]
+    sources = (ids_in, cell_in, frac_in) + tuple(moved_in)
+    copies = [
+        pltpu.make_async_copy(source, held, sems.at[n])
+        for n, (source, held) in enumerate(zip(sources, (ids_ref, cell_ref, frac_ref) + tuple(moved_out)))
+    ]
+    for copy in copies:
+        copy.start()
+    copies[0].wait()
     crossed, rays = ids_ref.shape
     fields, _, samples, _ = cell_ref.shape
     bricks = lb * devices
@@ -43,11 +56,14 @@
         named.astype(BF16), earlier.astype(F32).astype(BF16), preferred_element_type=F32
     )
     coord_ref[...] = jnp.zeros(coord_ref.shape, F32)
+    copies[1].wait()
+    copies[2].wait()
     shift = lb.bit_length() - 1
     device_rows = row_iota((devices, rays))
     hots, slots = [], [[], [], []]
     span = fields * 4
-    pad = out_ref.shape[1] - lb * cap * span
+    halves = out_ref.shape[0] // devices
+    pad = halves * 128 - lb * cap * span
     for c in range(crossed):
         rank = jnp.sum(jnp.where(member[c], before, 0.0), axis=0, keepdims=True).astype(jnp.int32)
         device = lax.shift_right_logical(ids[c], shift)
@@ -69,7 +85,10 @@
     for n in range(3):
         part = dot_t(hot, jnp.concatenate(slots[n], axis=1))
         total = part if total is None else total + part
-    out_ref[...] = total
+    for h in range(halves):
+        out_ref[pl.ds(h, devices, stride=halves), :] = total[:, h * 128 : h * 128 + 128]
+    for copy in copies[3:]:
+        copy.wait()
 
 
 def hat(value, place):
@@ -82,58 +101,55 @@
 
 def forward_kernel(
     arrived_ref, planes_ref, first_ref, last_ref, out_ref, table_ref, feature_ref, hidden_ref,
-    slope_ref, turned_ref, rows_ref, result_ref, *, lb, cap, samples
-):
-    cells = planes_ref.shape[2]
+    slope_ref, turned_ref, rows_ref, result_ref, *, lb, cap, samples, lanes
+):
+    orients, cells = planes_ref.shape[1:3]
     side = math.isqrt(cells)
-    lanes = arrived_ref.shape[0]
-    brick = pl.program_id(0)
     span = 24
-    orients = planes_ref.shape[1]
-
-    @pl.when(brick == 0)
-    def _():
-        turned_ref[...] = arrived_ref[...].T
-        result_ref[...] = jnp.zeros(result_ref.shape, F32)
-
-    rows_ref[...] = turned_ref[pl.ds(pl.multiple_of(brick * (cap * span), 8), cap * span), :]
+    halves = arrived_ref.shape[0] // lanes
+    for h in range(halves):
+        turned_ref[h * 128 : h * 128 + 128, :] = arrived_ref[pl.ds(h, lanes, stride=halves), :].T
+    result_ref[...] = jnp.zeros(result_ref.shape, F32)
     place = row_iota((side, lanes)).astype(F32)
-    for k in range(cap):
-        for s in range(samples):
-            block = (k * samples + s) * lanes
-            for p in range(orients):
-                at = k * span + 8 * p + s
-                x = jnp.broadcast_to(rows_ref[at : at + 1, :], (side, lanes))
-                y = jnp.broadcast_to(rows_ref[at + 4 : at + 5, :], (side, lanes))
-                across = hat(y, place)
-                for a in range(side):
-                    table_ref[0, p * cells + a * side : p * cells + (a + 1) * side, block : block + lanes] = (
-                        hat(x, float(a)) * across
-                    ).astype(BF16)
-    planes_t = planes_ref[0].reshape(orients * cells, -1).T
-    feature = jnp.dot(planes_t, table_ref[0], preferred_element_type=F32).astype(BF16)
-    feature_ref[0] = feature
-    before = jnp.dot(first_ref[0].T, feature, preferred_element_type=F32)
-    hidden = jnp.maximum(before, 0.0).astype(BF16)
-    hidden_ref[0] = hidden
-    raw = jnp.dot(last_ref[0], hidden, preferred_element_type=F32)
-    gate = jax.nn.sigmoid(raw)
-    is_density = row_iota(raw.shape) == 0
-    result = jnp.where(is_density, jax.nn.softplus(raw), gate)
-    slope_ref[0] = jnp.where(is_density, gate, gate * (1.0 - gate))
-    for b in range(lb):
-
-        @pl.when(brick == b)
-        def _(b=b):
-            for k in range(cap):
-                for s in range(samples):
-                    block = (k * samples + s) * lanes
-                    row = result_row(b * cap + k, s, lb, cap)
-                    result_ref[row : row + 4, :] = result[:, block : block + lanes]
-
-    @pl.when(brick == lb - 1)
-    def _():
-        out_ref[...] = result_ref[...].T
+
+    @pl.loop(0, lb)
+    def _(brick):
+        rows_ref[...] = turned_ref[pl.ds(pl.multiple_of(brick * (cap * span), 8), cap * span), :]
+        for k in range(cap):
+            for s in range(samples):
+                block = (k * samples + s) * lanes
+                for p in range(orients):
+                    at = k * span + 8 * p + s
+                    x = jnp.broadcast_to(rows_ref[at : at + 1, :], (side, lanes))
+                    y = jnp.broadcast_to(rows_ref[at + 4 : at + 5, :], (side, lanes))
+                    across = hat(y, place)
+                    for a in range(side):
+                        start = p * cells + a * side
+                        table_ref[brick, start : start + side, block : block + lanes] = (
+                            hat(x, float(a)) * across
+                        ).astype(BF16)
+        planes_t = planes_ref[brick].reshape(orients * cells, -1).T
+        feature = jnp.dot(planes_t, table_ref[brick], preferred_element_type=F32).astype(BF16)
+        feature_ref[brick] = feature
+        before = jnp.dot(first_ref[brick].T, feature, preferred_element_type=F32)
+        hidden = jnp.maximum(before, 0.0).astype(BF16)
+        hidden_ref[brick] = hidden
+        raw = jnp.dot(last_ref[brick], hidden, preferred_element_type=F32)
+        gate = jax.nn.sigmoid(raw)
+        is_density = row_iota(raw.shape) == 0
+        result = jnp.where(is_density, jax.nn.softplus(raw), gate)
+        slope_ref[brick] = jnp.where(is_density, gate, gate * (1.0 - gate))
+        for b in range(lb):
+
+            @pl.when(brick == b)
+            def _(b=b):
+                for k in range(cap):
+                    for s in range(samples):
+                        block = (k * samples + s) * lanes
+                        row = result_row(b * cap + k, s, lb, cap)
+                        result_ref[row : row + 4, :] = result[:, block : block + lanes]
+
+    out_ref[...] = result_ref[...].T
 
 
 def render_kernel(
@@ -218,46 +234,59 @@
 
 def backward_kernel(
     arrived_ref, table_ref, feature_ref, hidden_ref, slope_ref, first_ref, last_ref,
-    plane_ref, first_grad_ref, last_grad_ref, turned_ref, cot_ref, *, lb, cap, samples
+    plane_out, first_out, last_out, turned_ref, cot_ref, plane_ref, first_grad_ref, last_grad_ref,
+    sems, *, lb, cap, samples
 ):
     lanes = arrived_ref.shape[0]
-    brick = pl.program_id(0)
-
-    @pl.when(brick == 0)
-    def _():
-        turned_ref[...] = arrived_ref[...].T
+    turned_ref[...] = arrived_ref[...].T
+    orients, cells, channels = plane_ref.shape[1:]
+    pairs = ((plane_ref, plane_out), (first_grad_ref, first_out), (last_grad_ref, last_out))
+
+    def copies(brick):
+        return [
+            pltpu.make_async_copy(held.at[brick], out.at[brick], sems.at[n, brick])
+            for n, (held, out) in enumerate(pairs)
+        ]
+
+    @pl.loop(0, lb)
+    def _(brick):
+        for b in range(lb):
+
+            @pl.when(brick == b)
+            def _(b=b):
+                for k in range(cap):
+                    for s in range(samples):
+                        block = (k * samples + s) * lanes
+                        row = result_row(b * cap + k, s, lb, cap)
+                        cot_ref[:, block : block + lanes] = turned_ref[row : row + 4, :]
+
+        raw_cot = (cot_ref[...] * slope_ref[brick]).astype(BF16)
+        hidden = hidden_ref[brick]
+        last_grad_ref[brick] = dot_t(raw_cot, hidden)
+        last_t = last_ref[brick].astype(F32).T.astype(BF16)
+        hidden_cot = jnp.dot(last_t, raw_cot, preferred_element_type=F32)
+        before_cot = jnp.where(hidden.astype(F32) > 0, hidden_cot, 0.0).astype(BF16)
+        first_grad_ref[brick] = dot_t(feature_ref[brick], before_cot)
+        feature_cot = jnp.dot(first_ref[brick], before_cot, preferred_element_type=F32).astype(BF16)
+        plane_ref[brick] = dot_t(table_ref[brick], feature_cot).reshape(orients, cells, channels)
+        for copy in copies(brick):
+            copy.start()
 
     for b in range(lb):
-
-        @pl.when(brick == b)
-        def _(b=b):
-            for k in range(cap):
-                for s in range(samples):
-                    block = (k * samples + s) * lanes
-                    row = result_row(b * cap + k, s, lb, cap)
-                    cot_ref[:, block : block + lanes] = turned_ref[row : row + 4, :]
-
-    raw_cot = (cot_ref[...] * slope_ref[0]).astype(BF16)
-    hidden = hidden_ref[0]
-    last_grad_ref[0] = dot_t(raw_cot, hidden)
-    hidden_cot = jnp.dot(last_ref[0].astype(F32).T.astype(BF16), raw_cot, preferred_element_type=F32)
-    before_cot = jnp.where(hidden.astype(F32) > 0, hidden_cot, 0.0).astype(BF16)
-    first_grad_ref[0] = dot_t(feature_ref[0], before_cot)
-    feature_cot = jnp.dot(first_ref[0], before_cot, preferred_element_type=F32).astype(BF16)
-    orients, cells, channels = plane_ref.shape[1:]
-    plane_ref[0] = dot_t(table_ref[0], feature_cot).reshape(orients, cells, channels)
+        for copy in copies(b):
+            copy.wait()
 
 
 def exchange(block):
     return lax.all_to_all(block, AXES, split_axis=0, concat_axis=0, tiled=True)
 
 
-def whole(shape):
-    return pl.BlockSpec(shape, lambda *_: (0,) * len(shape))
-
-
-def per_brick(shape):
-    return pl.BlockSpec((1,) + tuple(shape[1:]), lambda b: (b,) + (0,) * (len(shape) - 1))
+def in_vmem(value):
+    return pltpu.with_memory_space_constraint(value, pltpu.VMEM)
+
+
+def params(mib):
+    return pltpu.CompilerParams(vmem_limit_bytes=mib << 20)
 
 
 def on_device(
@@ -276,60 +305,66 @@
     rows = cap * samples * devices
     shape = jax.ShapeDtypeStruct
 
-    outgoing, route = pl.pallas_call(
+    moved = (planes, first_layer, last_layer, step_length, target)
+    staged = (brick_ids.T, cell_index, cell_frac)
+    outgoing, route, *moved = pl.pallas_call(
         lambda *refs: scatter_kernel(*refs, lb=lb, cap=cap, devices=devices),
-        out_shape=(shape((devices, width), F32), shape((8, rays), jnp.int32)),
-        scratch_shapes=[pltpu.VMEM((crossed, fields * 4, rays), F32)],
+        in_specs=[pl.BlockSpec(memory_space=pltpu.HBM)] * (len(staged) + len(moved)),
+        out_shape=(pltpu.VMEM((devices * width // 128, 128), F32), pltpu.VMEM((8, rays), jnp.int32))
+        + tuple(pltpu.VMEM(m.shape, m.dtype) for m in moved),
+        scratch_shapes=[pltpu.VMEM(m.shape, m.dtype) for m in staged]
+        + [
+            pltpu.VMEM((crossed, fields * 4, rays), F32),
+            pltpu.SemaphoreType.DMA((len(staged) + len(moved),)),
+        ],
+        compiler_params=params(8),
         name="scatter",
-    )(brick_ids.T, cell_index, cell_frac)
+    )(*(pltpu.with_memory_space_constraint(m, pltpu.HBM) for m in staged + moved))
+    planes, first_layer, last_layer, step_length, target = map(in_vmem, moved)
     arrived = exchange(outgoing)
 
-    saved = (
-        shape((lb, orients * cells, rows), BF16),
-        shape((lb, channels, rows), BF16),
-        shape((lb, hidden_units, rows), BF16),
-        shape((lb, 4, rows), F32),
-    )
     results, table, feature, hidden, slope = pl.pallas_call(
-        lambda *refs: forward_kernel(*refs, lb=lb, cap=cap, samples=samples),
-        grid=(lb,),
-        in_specs=[
-            whole(arrived.shape), per_brick(planes.shape), per_brick(first_layer.shape),
-            per_brick(last_layer.shape),
-        ],
-        out_specs=(whole((devices, back)),) + tuple(per_brick(s.shape) for s in saved),
-        out_shape=(shape((devices, back), F32),) + saved,
+        lambda *refs: forward_kernel(*refs, lb=lb, cap=cap, samples=samples, lanes=devices),
+        out_shape=(
+            pltpu.VMEM((devices, back), F32),
+            pltpu.VMEM((lb, orients * cells, rows), BF16),
+            pltpu.VMEM((lb, channels, rows), BF16),
+            pltpu.VMEM((lb, hidden_units, rows), BF16),
+            pltpu.VMEM((lb, 4, rows), F32),
+        ),
         scratch_shapes=[
             pltpu.VMEM((width, devices), F32),
             pltpu.VMEM((cap * fields * 4, devices), F32),
             pltpu.VMEM((back, devices), F32),
         ],
+        compiler_params=params(24),
         name="forward",
-    )(arrived, planes, first_layer, last_layer)
+    )(in_vmem(arrived), planes, first_layer, last_layer)
     returned = exchange(results)
 
     colour, cot_out = pl.pallas_call(
         lambda *refs: render_kernel(*refs, lb=lb, cap=cap),
-        out_shape=(shape(target.shape, F32), shape((devices, back), F32)),
+        out_shape=(shape(target.shape, F32), pltpu.VMEM((devices, back), F32)),
+        compiler_params=params(8),
         name="render",
-    )(returned, route, step_length, target)
+    )(in_vmem(returned), in_vmem(route), step_length, target)
     cot_in = exchange(cot_out)
 
     grads = (
-        shape(planes.shape, F32),
-        shape(first_layer.shape, F32),
-        shape(last_layer.shape, F32),
+        shape((lb, orients, cells, channels), F32),
+        shape((lb, channels, hidden_units), F32),
+        shape((lb, 4, hidden_units), F32),
     )
     plane_grad, first_grad, last_grad = pl.pallas_call(
         lambda *refs: backward_kernel(*refs, lb=lb, cap=cap, samples=samples),
-        grid=(lb,),
-        in_specs=[whole(cot_in.shape)] + [per_brick(s.shape) for s in saved]
-        + [per_brick(first_layer.shape), per_brick(last_layer.shape)],
-        out_specs=tuple(per_brick(s.shape) for s in grads),
+        out_specs=tuple(pl.BlockSpec(memory_space=pl.ANY) for _ in grads),
         out_shape=grads,
-        scratch_shapes=[pltpu.VMEM((back, devices), F32), pltpu.VMEM((4, rows), F32)],
+        scratch_shapes=[pltpu.VMEM((back, devices), F32), pltpu.VMEM((4, rows), F32)]
+        + [pltpu.VMEM(g.shape, F32) for g in grads]
+        + [pltpu.SemaphoreType.DMA((len(grads), lb))],
+        compiler_params=params(24),
         name="backward",
-    )(cot_in, table, feature, hidden, slope, first_layer, last_layer)
+    )(in_vmem(cot_in), *map(in_vmem, (table, feature, hidden, slope)), first_layer, last_layer)
     return colour, plane_grad, first_grad, last_grad
 
 

time: 72.8 us -> 61.1 us (0.84)
  Pallas kernels: 18.8 us -> 11.3 us
  blocking collectives: 51.3 us -> 48.9 us
  local copies, waits for them, and re-layouts: 1.7 us -> 0 us
    pallas_call x1, Pallas kernels: 7.44 us -> 4.08 us  [on_device(): pl.pallas_call(lambda *refs: forward_kernel(*refs, lb=lb, cap=cap, sample...]
    all_to_all x3, blocking collectives: 51.3 us -> 48.9 us  [exchange(): return lax.all_to_all(block, AXES, split_axis=0, concat_axis=0, tiled=True)]
    pallas_call x1, Pallas kernels: 7.22 us -> 4.94 us  [on_device(): pl.pallas_call(lambda *refs: backward_kernel(*refs, lb=lb, cap=cap, sampl...]
    pallas_call x1, Pallas kernels: 2.14 us -> 0.96 us  [on_device(): pl.pallas_call(lambda *refs: render_kernel(*refs, lb=lb, cap=cap), out_sh...]
    all_to_all x1 -> x0, local copies, waits for them, and re-layouts: 1.04 us -> none  [exchange(): return lax.all_to_all(block, AXES, split_axis=0, concat_axis=0, tiled=True)]
where the time goes in v1:
time: 61.1 us; the launch traced here: 60.9 us
  blocking collectives  48.9 us (80%)
  Pallas kernels  11.3 us (18%)
  between operations  0.65 us (1%)
    all_to_all x3, blocking collectives, exchange(): return lax.all_to_all(block, AXES, split_axis=0, concat_axis=0, tiled=True)  48.9 us
    pallas_call x1, Pallas kernels, on_device(): pl.pallas_call(lambda *refs: backward_kernel(*refs, lb=lb, cap=cap, sampl...  4.94 us
    pallas_call x1, Pallas kernels, on_device(): pl.pallas_call(lambda *refs: forward_kernel(*refs, lb=lb, cap=cap, sample...  4.08 us
    pallas_call x1, Pallas kernels, on_device(): pl.pallas_call(lambda *refs: scatter_kernel(*refs, lb=lb, cap=cap, device...  1.34 us

profile of v1, /device:TPU:1, one launch (start us, length us, event | category | flops | bytes accessed | tf_op | source)
XLA Modules:
  0.0 60.9 jit_solution(13518142146361045432)
XLA Ops:
  0.6 1.3 %scatter.1 = (f32[256,128]{1,0:T(8,128)S(1)}, s32[8,128]{1,0:T(8,128)S(1)}, bf16[2,3,256,128]{3,2,1,0:T(8,128)(2,1)S(1)}, bf16[2,128,256]{2,1,0:T(8,128)(2,1)S(1...) custom-call(s32[3,128]{1,0:T(4,128)} %bitcast.17, s32[6,3,3,128]{3,2,1,0:T(4,128)} %refs_1_.1, ...), custom_call_target="tpu_custom_call" | custom-call | tf_op jit(solution)/shard_map/scatter/pallas_call | solution.py:310
  2.0 21.4 %all_to_all.33 = f32[128,2,128]{2,1,0:T(2,128)S(1)} all-to-all(f32[128,2,128]{2,1,0:T(2,128)S(1)} %bitcast.14), channel_id=1, replica_groups=mesh['bx'=16,'by'=8] {'bx','by'}, dimensions={0} | all-to-all | bytes 262144 | tf_op jit(solution)/shard_map/all_to_all | solution.py:281
  23.4 4.1 %forward.1 = (f32[128,128]{1,0:T(8,128)S(1)}, bf16[2,768,1920]{2,1,0:T(8,128)(2,1)S(1)}, bf16[2,128,1920]{2,1,0:T(8,128)(2,1)S(1)}, bf16[2,256,1920]{2,1,0:T(8,128)(2,1)S(1)}, f32[2,4,1920]{2,1,0:T(4,128)S(1)}) custom-call(f32[256,128]{1,0:T(8,128)S(1)} %bitcast.11, bf16[2,3,256,128]{3,2,1,0:T(8,128)(2,1)S(1)} %get-tuple-element.22.refs_1_, ...), custom_call_target="tpu_custom_call" | custom-call | tf_op jit(solution)/shard_map/forward/pallas_call | solution.py:326
  27.5 13.7 %all_to_all.34 = f32[128,1,128]{2,1,0:T(1,128)S(1)} all-to-all(f32[128,1,128]{2,1,0:T(1,128)S(1)} %bitcast.15), channel_id=1, replica_groups=mesh['bx'=16,'by'=8] {'bx','by'}, dimensions={0} | all-to-all | bytes 131072 | tf_op jit(solution)/shard_map/all_to_all | solution.py:281
  41.2 1.0 %render.1 = (f32[3,128]{1,0:T(4,128)}, f32[128,128]{1,0:T(8,128)S(1)}) custom-call(f32[128,128]{1,0:T(8,128)S(1)} %bitcast.13, s32[8,128]{1,0:T(8,128)S(1)} %get-tuple-element.26.refs_1_, f32[3,3,128]{2,1,0:T(4,128)S(1)} %get-tuple-element.27.refs_2_, f32[3,128]{1,0:T(4,128)S(1)} %get-tuple-element.28.refs_3_), custom_call_target="tpu_custom_call" | custom-call | tf_op jit(solution)/shard_map/render/pallas_call | solution.py:345
  42.1 13.8 %all_to_all.35 = f32[128,1,128]{2,1,0:T(1,128)S(1)} all-to-all(f32[128,1,128]{2,1,0:T(1,128)S(1)} %bitcast.16), channel_id=1, replica_groups=mesh['bx'=16,'by'=8] {'bx','by'}, dimensions={0} | all-to-all | bytes 131072 | tf_op jit(solution)/shard_map/all_to_all | solution.py:281
  56.0 4.9 %backward.1 = (f32[2,3,256,128]{3,2,1,0:T(8,128)}, f32[2,128,256]{2,1,0:T(8,128)}, f32[2,4,256]{2,1,0:T(4,128)}) custom-call(f32[128,128]{1,0:T(8,128)S(1)} %bitcast.12, bf16[2,768,1920]{2,1,0:T(8,128)(2,1)S(1)} %get-tuple-element.31.refs_1_, bf16[2,128,1920]{2,1,0:T(8,128)(2,1)S(1)} %get-tuple-element.32.refs_2_, ...), custom_call_target="tpu_custom_call" | custom-call | tf_op jit(solution)/shard_map/backward/pallas_call | solution.py:358

commit v2 on v1

--- a/solution.py
+++ b/solution.py
@@ -10,6 +10,7 @@
 F32 = jnp.float32
 BF16 = jnp.bfloat16
 AXES = ("bx", "by")
+CHUNK = 15
 
 
 def pieces_of(value):
@@ -67,7 +68,7 @@
     for c in range(crossed):
         rank = jnp.sum(jnp.where(member[c], before, 0.0), axis=0, keepdims=True).astype(jnp.int32)
         device = lax.shift_right_logical(ids[c], shift)
-        slot = (ids[c] & (lb - 1)) * cap + rank
+        slot = (ids[c] & (lb - 1)) * 8 + rank
         route_ref[c : c + 1, :] = device
         route_ref[4 + c : 5 + c, :] = slot
         hots.append((device_rows == jnp.broadcast_to(device, (devices, rays))).astype(F32).astype(BF16))
@@ -75,7 +76,7 @@
             coord_ref[c, f * 4 : f * 4 + samples, :] = cell_ref[f, c].astype(F32) + frac_ref[f, c]
         value = coord_ref[c]
         here = jnp.broadcast_to(slot, (span, rays))
-        rows = [jnp.where(here == q, value, 0.0) for q in range(lb * cap)]
+        rows = [jnp.where(here == b * 8 + k, value, 0.0) for b in range(lb) for k in range(cap)]
         if pad:
             rows.append(jnp.zeros((pad, rays), F32))
         for n, part in enumerate(pieces_of(jnp.concatenate(rows, axis=0))):
@@ -95,13 +96,17 @@
     return jnp.maximum(0.0, 1.0 - jnp.abs(value - place))
 
 
-def result_row(q, s, lb, cap):
-    return q * 8 + s * 4 if s < 2 else lb * cap * 8 + q * 4
+def result_row(k, s, cap):
+    return k * 8 + s * 4 if s < 2 else cap * 8 + k * 4
+
+
+def chunks_of(blocks, size):
+    return [(n, min(size, blocks - n)) for n in range(0, blocks, size)]
 
 
 def forward_kernel(
     arrived_ref, planes_ref, first_ref, last_ref, out_ref, table_ref, feature_ref, hidden_ref,
-    slope_ref, turned_ref, rows_ref, result_ref, *, lb, cap, samples, lanes
+    slope_ref, turned_ref, hat_ref, result_ref, *, lb, cap, samples, lanes
 ):
     orients, cells = planes_ref.shape[1:3]
     side = math.isqrt(cells)
@@ -112,44 +117,39 @@
     result_ref[...] = jnp.zeros(result_ref.shape, F32)
     place = row_iota((side, lanes)).astype(F32)
 
-    @pl.loop(0, lb)
-    def _(brick):
-        rows_ref[...] = turned_ref[pl.ds(pl.multiple_of(brick * (cap * span), 8), cap * span), :]
-        for k in range(cap):
-            for s in range(samples):
-                block = (k * samples + s) * lanes
+    for brick in range(lb):
+        planes_t = planes_ref[brick].reshape(orients * cells, -1).T
+        first_t = first_ref[brick].T
+        for begin, count in chunks_of(cap * samples, CHUNK):
+            for n in range(begin, begin + count):
+                k, s = divmod(n, samples)
                 for p in range(orients):
-                    at = k * span + 8 * p + s
-                    x = jnp.broadcast_to(rows_ref[at : at + 1, :], (side, lanes))
-                    y = jnp.broadcast_to(rows_ref[at + 4 : at + 5, :], (side, lanes))
-                    across = hat(y, place)
+                    at = (brick * cap + k) * span + 8 * p + s
+                    hat_ref[brick, n, p] = hat(jnp.broadcast_to(turned_ref[at : at + 1, :], (side, lanes)), place)
+                    across = hat(jnp.broadcast_to(turned_ref[at + 4 : at + 5, :], (side, lanes)), place)
                     for a in range(side):
                         start = p * cells + a * side
-                        table_ref[brick, start : start + side, block : block + lanes] = (
-                            hat(x, float(a)) * across
+                        along = jnp.broadcast_to(hat_ref[brick, n, p, a : a + 1, :], (side, lanes))
+                        table_ref[brick, start : start + side, n * lanes : (n + 1) * lanes] = (
+                            along * across
                         ).astype(BF16)
-        planes_t = planes_ref[brick].reshape(orients * cells, -1).T
-        feature = jnp.dot(planes_t, table_ref[brick], preferred_element_type=F32).astype(BF16)
-        feature_ref[brick] = feature
-        before = jnp.dot(first_ref[brick].T, feature, preferred_element_type=F32)
-        hidden = jnp.maximum(before, 0.0).astype(BF16)
-        hidden_ref[brick] = hidden
-        raw = jnp.dot(last_ref[brick], hidden, preferred_element_type=F32)
-        gate = jax.nn.sigmoid(raw)
-        is_density = row_iota(raw.shape) == 0
-        result = jnp.where(is_density, jax.nn.softplus(raw), gate)
-        slope_ref[brick] = jnp.where(is_density, gate, gate * (1.0 - gate))
-        for b in range(lb):
-
-            @pl.when(brick == b)
-            def _(b=b):
-                for k in range(cap):
-                    for s in range(samples):
-                        block = (k * samples + s) * lanes
-                        row = result_row(b * cap + k, s, lb, cap)
-                        result_ref[row : row + 4, :] = result[:, block : block + lanes]
-
-    out_ref[...] = result_ref[...].T
+            part = slice(begin * lanes, (begin + count) * lanes)
+            feature = jnp.dot(planes_t, table_ref[brick, :, part], preferred_element_type=F32).astype(BF16)
+            feature_ref[brick, :, part] = feature
+            before = jnp.dot(first_t, feature, preferred_element_type=F32)
+            hidden = jnp.maximum(before, 0.0).astype(BF16)
+            hidden_ref[brick, :, part] = hidden
+            raw = jnp.dot(last_ref[brick], hidden, preferred_element_type=F32)
+            gate = jax.nn.sigmoid(raw)
+            is_density = row_iota(raw.shape) == 0
+            result = jnp.where(is_density, jax.nn.softplus(raw), gate)
+            slope_ref[brick, :, part] = jnp.where(is_density, gate, gate * (1.0 - gate))
+            for n in range(begin, begin + count):
+                k, s = divmod(n, samples)
+                row = result_row(k, s, cap)
+                result_ref[brick, row : row + 4, :] = result[:, (n - begin) * lanes : (n - begin + 1) * lanes]
+
+    out_ref[...] = result_ref[...].reshape(out_ref.shape[1], lanes).T
 
 
 def render_kernel(
@@ -157,7 +157,6 @@
 ):
     devices = returned_ref.shape[0]
     crossed, samples, rays = step_ref.shape
-    slots = lb * cap
     turned = returned_ref[...].T
     parts = pieces_of(turned)
     device_rows = row_iota((devices, rays))
@@ -176,13 +175,14 @@
         slot = jnp.broadcast_to(route_ref[4 + c : 5 + c, :], (8, rays))
         block = fetched[:, c * rays : (c + 1) * rays]
         two = jnp.zeros((8, rays), F32)
-        for q in range(slots):
-            two = two + jnp.where(slot == q, block[q * 8 : q * 8 + 8], 0.0)
         third = jnp.zeros((8, rays), F32)
-        for h in range(slots // 2):
-            at = slots * 8 + h * 8
-            held = slot == parity + 2 * h
-            third = third + jnp.where(held, block[at : at + 8], 0.0)
+        for b in range(lb):
+            for k in range(cap):
+                at = b * 64 + k * 8
+                two = two + jnp.where(slot == b * 8 + k, block[at : at + 8], 0.0)
+            for k in range(0, cap, 2):
+                at = b * 64 + cap * 8 + k * 4
+                third = third + jnp.where(slot == parity + (b * 8 + k), block[at : at + 8], 0.0)
         third = third[0:4] + third[4:8]
         picked += [two[0:4], two[4:8], third]
     steps = [step_ref[c, s : s + 1, :] for c in range(crossed) for s in range(samples)]
@@ -217,12 +217,10 @@
         slot = jnp.broadcast_to(route_ref[4 + c : 5 + c, :], (8, rays))
         two = jnp.concatenate([cots[c * samples], cots[c * samples + 1]], axis=0)
         third = jnp.concatenate([cots[c * samples + 2]] * 2, axis=0)
-        rows = [jnp.where(slot == q, two, 0.0) for q in range(slots)]
-        for h in range(slots // 2):
-            rows.append(jnp.where(slot == parity + 2 * h, third, 0.0))
-        pad = out_ref.shape[1] - slots * 12
-        if pad:
-            rows.append(jnp.zeros((pad, rays), F32))
+        rows = []
+        for b in range(lb):
+            rows += [jnp.where(slot == b * 8 + k, two, 0.0) for k in range(cap)]
+            rows += [jnp.where(slot == parity + (b * 8 + k), third, 0.0) for k in range(0, cap, 2)]
         for n, part in enumerate(pieces_of(jnp.concatenate(rows, axis=0))):
             placed[n].append(part)
     total = None
@@ -234,47 +232,54 @@
 
 def backward_kernel(
     arrived_ref, table_ref, feature_ref, hidden_ref, slope_ref, first_ref, last_ref,
-    plane_out, first_out, last_out, turned_ref, cot_ref, plane_ref, first_grad_ref, last_grad_ref,
+    plane_out, first_out, last_out, turned_ref, raw_cot_ref, before_cot_ref, feature_cot_ref, plane_ref, first_grad_ref, last_grad_ref,
     sems, *, lb, cap, samples
 ):
     lanes = arrived_ref.shape[0]
-    turned_ref[...] = arrived_ref[...].T
+    turned_ref[...] = arrived_ref[...].T.reshape(turned_ref.shape)
     orients, cells, channels = plane_ref.shape[1:]
     pairs = ((plane_ref, plane_out), (first_grad_ref, first_out), (last_grad_ref, last_out))
 
-    def copies(brick):
-        return [
-            pltpu.make_async_copy(held.at[brick], out.at[brick], sems.at[n, brick])
-            for n, (held, out) in enumerate(pairs)
-        ]
-
-    @pl.loop(0, lb)
-    def _(brick):
-        for b in range(lb):
-
-            @pl.when(brick == b)
-            def _(b=b):
-                for k in range(cap):
-                    for s in range(samples):
-                        block = (k * samples + s) * lanes
-                        row = result_row(b * cap + k, s, lb, cap)
-                        cot_ref[:, block : block + lanes] = turned_ref[row : row + 4, :]
-
-        raw_cot = (cot_ref[...] * slope_ref[brick]).astype(BF16)
-        hidden = hidden_ref[brick]
-        last_grad_ref[brick] = dot_t(raw_cot, hidden)
+    copies = []
+
+    def send(n, brick, *part):
+        held, out = pairs[n]
+        copies.append(
+            pltpu.make_async_copy(held.at[(brick,) + part], out.at[(brick,) + part], sems.at[len(copies)])
+        )
+        copies[-1].start()
+
+    def over_halves(a, b):
+        half = -(-a.shape[1] // 512) * 256
+        return dot_t(a[:, :half], b[:, :half]) + dot_t(a[:, half:], b[:, half:])
+
+    for brick in range(lb):
         last_t = last_ref[brick].astype(F32).T.astype(BF16)
-        hidden_cot = jnp.dot(last_t, raw_cot, preferred_element_type=F32)
-        before_cot = jnp.where(hidden.astype(F32) > 0, hidden_cot, 0.0).astype(BF16)
-        first_grad_ref[brick] = dot_t(feature_ref[brick], before_cot)
-        feature_cot = jnp.dot(first_ref[brick], before_cot, preferred_element_type=F32).astype(BF16)
-        plane_ref[brick] = dot_t(table_ref[brick], feature_cot).reshape(orients, cells, channels)
-        for copy in copies(brick):
-            copy.start()
-
-    for b in range(lb):
-        for copy in copies(b):
-            copy.wait()
+        for begin, count in chunks_of(cap * samples, CHUNK):
+            part = slice(begin * lanes, (begin + count) * lanes)
+            cots = []
+            for n in range(begin, begin + count):
+                k, s = divmod(n, samples)
+                row = result_row(k, s, cap)
+                cots.append(turned_ref[brick, row : row + 4, :])
+            raw_cot = (jnp.concatenate(cots, axis=1) * slope_ref[brick, :, part]).astype(BF16)
+            raw_cot_ref[brick, :, part] = raw_cot
+            hidden_cot = jnp.dot(last_t, raw_cot, preferred_element_type=F32).astype(BF16)
+            zero = jnp.zeros((), BF16)
+            before_cot = jnp.where(hidden_ref[brick, :, part] > zero, hidden_cot, zero)
+            before_cot_ref[brick, :, part] = before_cot
+            feature_cot_ref[brick, :, part] = jnp.dot(
+                first_ref[brick], before_cot, preferred_element_type=F32
+            ).astype(BF16)
+    for brick in range(lb):
+        plane_ref[brick] = dot_t(table_ref[brick], feature_cot_ref[brick]).reshape(orients, cells, channels)
+        send(0, brick)
+        first_grad_ref[brick] = over_halves(feature_ref[brick], before_cot_ref[brick])
+        send(1, brick)
+        last_grad_ref[brick] = over_halves(raw_cot_ref[brick], hidden_ref[brick])
+        send(2, brick)
+    for copy in copies:
+        copy.wait()
 
 
 def exchange(block):
@@ -301,7 +306,7 @@
     cap = max(2, (3 * rays * crossed + bricks - 1) // bricks)
     fields = cell_index.shape[0]
     width = -(-lb * cap * fields * 4 // 128) * 128
-    back = -(-lb * cap * 12 // 128) * 128
+    back = lb * 64
     rows = cap * samples * devices
     shape = jax.ShapeDtypeStruct
 
@@ -334,8 +339,8 @@
         ),
         scratch_shapes=[
             pltpu.VMEM((width, devices), F32),
-            pltpu.VMEM((cap * fields * 4, devices), F32),
-            pltpu.VMEM((back, devices), F32),
+            pltpu.VMEM((lb, cap * samples, orients, math.isqrt(cells), devices), F32),
+            pltpu.VMEM((lb, 64, devices), F32),
         ],
         compiler_params=params(24),
         name="forward",
@@ -359,9 +364,14 @@
         lambda *refs: backward_kernel(*refs, lb=lb, cap=cap, samples=samples),
         out_specs=tuple(pl.BlockSpec(memory_space=pl.ANY) for _ in grads),
         out_shape=grads,
-        scratch_shapes=[pltpu.VMEM((back, devices), F32), pltpu.VMEM((4, rows), F32)]
+        scratch_shapes=[
+            pltpu.VMEM((lb, 64, devices), F32),
+            pltpu.VMEM((lb, 4, rows), BF16),
+            pltpu.VMEM((lb, hidden_units, rows), BF16),
+            pltpu.VMEM((lb, channels, rows), BF16),
+        ]
         + [pltpu.VMEM(g.shape, F32) for g in grads]
-        + [pltpu.SemaphoreType.DMA((len(grads), lb))],
+        + [pltpu.SemaphoreType.DMA((len(grads) * lb,))],
         compiler_params=params(24),
         name="backward",
     )(in_vmem(cot_in), *map(in_vmem, (table, feature, hidden, slope)), first_layer, last_layer)

time: 61.1 us -> 59.3 us (0.971)
  Pallas kernels: 11.3 us -> 9.52 us
    pallas_call x1, Pallas kernels: 4.08 us -> 2.76 us  [on_device(): pl.pallas_call(lambda *refs: forward_kernel(*refs, lb=lb, cap=cap, sample...]
where the time goes in v2:
time: 59.3 us; the launch traced here: 59.1 us
  blocking collectives  48.9 us (82%)
  Pallas kernels  9.52 us (16%)
  between operations  0.65 us (1%)
    all_to_all x3, blocking collectives, exchange(): return lax.all_to_all(block, AXES, split_axis=0, concat_axis=0, tiled=True)  48.9 us
    pallas_call x1, Pallas kernels, on_device(): pl.pallas_call(lambda *refs: backward_kernel(*refs, lb=lb, cap=cap, sampl...  4.47 us
    pallas_call x1, Pallas kernels, on_device(): pl.pallas_call(lambda *refs: forward_kernel(*refs, lb=lb, cap=cap, sample...  2.76 us
    pallas_call x1, Pallas kernels, on_device(): pl.pallas_call(lambda *refs: scatter_kernel(*refs, lb=lb, cap=cap, device...  1.34 us

profile of v2, /device:TPU:1, one launch (start us, length us, event | category | flops | bytes accessed | tf_op | source)
XLA Modules:
  0.0 59.1 jit_solution(9290879361439653741)
XLA Ops:
  0.6 1.3 %scatter.1 = (f32[256,128]{1,0:T(8,128)S(1)}, s32[8,128]{1,0:T(8,128)S(1)}, bf16[2,3,256,128]{3,2,1,0:T(8,128)(2,1)S(1)}, bf16[2,128,256]{2,1,0:T(8,128)(2,1)S(1...) custom-call(s32[3,128]{1,0:T(4,128)} %bitcast.17, s32[6,3,3,128]{3,2,1,0:T(4,128)} %refs_1_.1, ...), custom_call_target="tpu_custom_call" | custom-call | tf_op jit(solution)/shard_map/scatter/pallas_call | solution.py:315
  2.0 21.4 %all_to_all.33 = f32[128,2,128]{2,1,0:T(2,128)S(1)} all-to-all(f32[128,2,128]{2,1,0:T(2,128)S(1)} %bitcast.14), channel_id=1, replica_groups=mesh['bx'=16,'by'=8] {'bx','by'}, dimensions={0} | all-to-all | bytes 262144 | tf_op jit(solution)/shard_map/all_to_all | solution.py:286
  23.4 2.8 %forward.1 = (f32[128,128]{1,0:T(8,128)S(1)}, bf16[2,768,1920]{2,1,0:T(8,128)(2,1)S(1)}, bf16[2,128,1920]{2,1,0:T(8,128)(2,1)S(1)}, bf16[2,256,1920]{2,1,0:T(8,128)(2,1)S(1)}, f32[2,4,1920]{2,1,0:T(4,128)S(1)}) custom-call(f32[256,128]{1,0:T(8,128)S(1)} %bitcast.11, bf16[2,3,256,128]{3,2,1,0:T(8,128)(2,1)S(1)} %get-tuple-element.22.refs_1_, ...), custom_call_target="tpu_custom_call" | custom-call | tf_op jit(solution)/shard_map/forward/pallas_call | solution.py:331
  26.2 13.7 %all_to_all.34 = f32[128,1,128]{2,1,0:T(1,128)S(1)} all-to-all(f32[128,1,128]{2,1,0:T(1,128)S(1)} %bitcast.15), channel_id=1, replica_groups=mesh['bx'=16,'by'=8] {'bx','by'}, dimensions={0} | all-to-all | bytes 131072 | tf_op jit(solution)/shard_map/all_to_all | solution.py:286
  39.8 0.9 %render.1 = (f32[3,128]{1,0:T(4,128)}, f32[128,128]{1,0:T(8,128)S(1)}) custom-call(f32[128,128]{1,0:T(8,128)S(1)} %bitcast.13, s32[8,128]{1,0:T(8,128)S(1)} %get-tuple-element.26.refs_1_, f32[3,3,128]{2,1,0:T(4,128)S(1)} %get-tuple-element.27.refs_2_, f32[3,128]{1,0:T(4,128)S(1)} %get-tuple-element.28.refs_3_), custom_call_target="tpu_custom_call" | custom-call | tf_op jit(solution)/shard_map/render/pallas_call | solution.py:350
  40.8 13.8 %all_to_all.35 = f32[128,1,128]{2,1,0:T(1,128)S(1)} all-to-all(f32[128,1,128]{2,1,0:T(1,128)S(1)} %bitcast.16), channel_id=1, replica_groups=mesh['bx'=16,'by'=8] {'bx','by'}, dimensions={0} | all-to-all | bytes 131072 | tf_op jit(solution)/shard_map/all_to_all | solution.py:286
  54.6 4.5 %backward.1 = (f32[2,3,256,128]{3,2,1,0:T(8,128)}, f32[2,128,256]{2,1,0:T(8,128)}, f32[2,4,256]{2,1,0:T(4,128)}) custom-call(f32[128,128]{1,0:T(8,128)S(1)} %bitcast.12, bf16[2,768,1920]{2,1,0:T(8,128)(2,1)S(1)} %get-tuple-element.31.refs_1_, bf16[2,128,1920]{2,1,0:T(8,128)(2,1)S(1)} %get-tuple-element.32.refs_2_, ...), custom_call_target="tpu_custom_call" | custom-call | tf_op jit(solution)/shard_map/backward/pallas_call | solution.py:363

commit v3 on v2

--- a/solution.py
+++ b/solution.py
@@ -42,21 +42,20 @@
     ]
     for copy in copies:
         copy.start()
-    copies[0].wait()
     crossed, rays = ids_ref.shape
     fields, _, samples, _ = cell_ref.shape
     bricks = lb * devices
+    earlier = row_iota((rays, rays)) < lax.broadcasted_iota(jnp.int32, (rays, rays), 1)
+    earlier = earlier.astype(F32).astype(BF16)
+    coord_ref[...] = jnp.zeros(coord_ref.shape, F32)
+    copies[0].wait()
     ids = [ids_ref[c : c + 1, :] for c in range(crossed)]
     brick_rows = row_iota((bricks, rays))
     member = [brick_rows == jnp.broadcast_to(i, (bricks, rays)) for i in ids]
     named = member[0].astype(F32)
     for c in range(1, crossed):
         named = named + member[c].astype(F32)
-    earlier = row_iota((rays, rays)) < lax.broadcasted_iota(jnp.int32, (rays, rays), 1)
-    before = jnp.dot(
-        named.astype(BF16), earlier.astype(F32).astype(BF16), preferred_element_type=F32
-    )
-    coord_ref[...] = jnp.zeros(coord_ref.shape, F32)
+    before = jnp.dot(named.astype(BF16), earlier, preferred_element_type=F32)
     copies[1].wait()
     copies[2].wait()
     shift = lb.bit_length() - 1
@@ -231,16 +230,16 @@
 
 
 def backward_kernel(
-    arrived_ref, table_ref, feature_ref, hidden_ref, slope_ref, first_ref, last_ref,
-    plane_out, first_out, last_out, turned_ref, raw_cot_ref, before_cot_ref, feature_cot_ref, plane_ref, first_grad_ref, last_grad_ref,
+    arrived_ref, colour_ref, table_ref, feature_ref, hidden_ref, slope_ref, first_ref, last_ref,
+    colour_out, plane_out, first_out, last_out, turned_ref, raw_cot_ref, before_cot_ref, feature_cot_ref, plane_ref, first_grad_ref, last_grad_ref,
     sems, *, lb, cap, samples
 ):
     lanes = arrived_ref.shape[0]
+    copies = [pltpu.make_async_copy(colour_ref, colour_out, sems.at[0])]
+    copies[0].start()
     turned_ref[...] = arrived_ref[...].T.reshape(turned_ref.shape)
     orients, cells, channels = plane_ref.shape[1:]
     pairs = ((plane_ref, plane_out), (first_grad_ref, first_out), (last_grad_ref, last_out))
-
-    copies = []
 
     def send(n, brick, *part):
         held, out = pairs[n]
@@ -349,18 +348,19 @@
 
     colour, cot_out = pl.pallas_call(
         lambda *refs: render_kernel(*refs, lb=lb, cap=cap),
-        out_shape=(shape(target.shape, F32), pltpu.VMEM((devices, back), F32)),
+        out_shape=(pltpu.VMEM(target.shape, F32), pltpu.VMEM((devices, back), F32)),
         compiler_params=params(8),
         name="render",
     )(in_vmem(returned), in_vmem(route), step_length, target)
     cot_in = exchange(cot_out)
 
     grads = (
+        shape(target.shape, F32),
         shape((lb, orients, cells, channels), F32),
         shape((lb, channels, hidden_units), F32),
         shape((lb, 4, hidden_units), F32),
     )
-    plane_grad, first_grad, last_grad = pl.pallas_call(
+    return pl.pallas_call(
         lambda *refs: backward_kernel(*refs, lb=lb, cap=cap, samples=samples),
         out_specs=tuple(pl.BlockSpec(memory_space=pl.ANY) for _ in grads),
         out_shape=grads,
@@ -370,12 +370,11 @@
             pltpu.VMEM((lb, hidden_units, rows), BF16),
             pltpu.VMEM((lb, channels, rows), BF16),
         ]
-        + [pltpu.VMEM(g.shape, F32) for g in grads]
-        + [pltpu.SemaphoreType.DMA((len(grads) * lb,))],
+        + [pltpu.VMEM(g.shape, F32) for g in grads[1:]]
+        + [pltpu.SemaphoreType.DMA((1 + 3 * lb,))],
         compiler_params=params(24),
         name="backward",
-    )(in_vmem(cot_in), *map(in_vmem, (table, feature, hidden, slope)), first_layer, last_layer)
-    return colour, plane_grad, first_grad, last_grad
+    )(*map(in_vmem, (cot_in, colour, table, feature, hidden, slope)), first_layer, last_layer)
 
 
 def solution(mesh):

time: 59.3 us -> 59 us (level)
  no operation moved by 1% of the time
where the time goes in v3:
time: 59 us; the launch traced here: 58.8 us
  blocking collectives  48.9 us (83%)
  Pallas kernels  9.22 us (16%)
  between operations  0.66 us (1%)
    all_to_all x3, blocking collectives, exchange(): return lax.all_to_all(block, AXES, split_axis=0, concat_axis=0, tiled=True)  48.9 us
    pallas_call x1, Pallas kernels, on_device(): pl.pallas_call(lambda *refs: backward_kernel(*refs, lb=lb, cap=cap, sampl...  4.48 us
    pallas_call x1, Pallas kernels, on_device(): pl.pallas_call(lambda *refs: forward_kernel(*refs, lb=lb, cap=cap, sample...  2.76 us
    pallas_call x1, Pallas kernels, on_device(): pl.pallas_call(lambda *refs: scatter_kernel(*refs, lb=lb, cap=cap, device...  1.34 us

profile of v3, /device:TPU:1, one launch (start us, length us, event | category | flops | bytes accessed | tf_op | source)
XLA Modules:
  0.0 58.8 jit_solution(2972875354891916615)
XLA Ops:
  0.6 1.3 %scatter.1 = (f32[256,128]{1,0:T(8,128)S(1)}, s32[8,128]{1,0:T(8,128)S(1)}, bf16[2,3,256,128]{3,2,1,0:T(8,128)(2,1)S(1)}, bf16[2,128,256]{2,1,0:T(8,128)(2,1)S(1...) custom-call(s32[3,128]{1,0:T(4,128)} %bitcast.17, s32[6,3,3,128]{3,2,1,0:T(4,128)} %refs_1_.1, ...), custom_call_target="tpu_custom_call" | custom-call | tf_op jit(solution)/shard_map/scatter/pallas_call | solution.py:314
  2.0 21.4 %all_to_all.33 = f32[128,2,128]{2,1,0:T(2,128)S(1)} all-to-all(f32[128,2,128]{2,1,0:T(2,128)S(1)} %bitcast.14), channel_id=1, replica_groups=mesh['bx'=16,'by'=8] {'bx','by'}, dimensions={0} | all-to-all | bytes 262144 | tf_op jit(solution)/shard_map/all_to_all | solution.py:285
  23.4 2.8 %forward.1 = (f32[128,128]{1,0:T(8,128)S(1)}, bf16[2,768,1920]{2,1,0:T(8,128)(2,1)S(1)}, bf16[2,128,1920]{2,1,0:T(8,128)(2,1)S(1)}, bf16[2,256,1920]{2,1,0:T(8,128)(2,1)S(1)}, f32[2,4,1920]{2,1,0:T(4,128)S(1)}) custom-call(f32[256,128]{1,0:T(8,128)S(1)} %bitcast.11, bf16[2,3,256,128]{3,2,1,0:T(8,128)(2,1)S(1)} %get-tuple-element.19.refs_1_, ...), custom_call_target="tpu_custom_call" | custom-call | tf_op jit(solution)/shard_map/forward/pallas_call | solution.py:330
  26.2 13.7 %all_to_all.34 = f32[128,1,128]{2,1,0:T(1,128)S(1)} all-to-all(f32[128,1,128]{2,1,0:T(1,128)S(1)} %bitcast.15), channel_id=1, replica_groups=mesh['bx'=16,'by'=8] {'bx','by'}, dimensions={0} | all-to-all | bytes 131072 | tf_op jit(solution)/shard_map/all_to_all | solution.py:285
  39.8 0.6 %render.1 = (f32[3,128]{1,0:T(4,128)S(1)}, f32[128,128]{1,0:T(8,128)S(1)}) custom-call(f32[128,128]{1,0:T(8,128)S(1)} %bitcast.13, s32[8,128]{1,0:T(8,128)S(1)} %get-tuple-element.23.refs_1_, f32[3,3,128]{2,1,0:T(4,128)S(1)} %get-tuple-element.24.refs_2_, f32[3,128]{1,0:T(4,128)S(1)} %get-tuple-element.25.refs_3_), custom_call_target="tpu_custom_call" | custom-call | tf_op jit(solution)/shard_map/render/pallas_call | solution.py:349
  40.5 13.8 %all_to_all.35 = f32[128,1,128]{2,1,0:T(1,128)S(1)} all-to-all(f32[128,1,128]{2,1,0:T(1,128)S(1)} %bitcast.16), channel_id=1, replica_groups=mesh['bx'=16,'by'=8] {'bx','by'}, dimensions={0} | all-to-all | bytes 131072 | tf_op jit(solution)/shard_map/all_to_all | solution.py:285
  54.3 4.5 %backward.1 = (f32[3,128]{1,0:T(4,128)}, f32[2,3,256,128]{3,2,1,0:T(8,128)}, f32[2,128,256]{2,1,0:T(8,128)}, f32[2,4,256]{2,1,0:T(4,128)}) custom-call(f32[128,128]{1,0:T(8,128)S(1)} %bitcast.12, f32[3,128]{1,0:T(4,128)S(1)} %get-tuple-element.27.refs_1_, bf16[2,768,1920]{2,1,0:T(8,128)(2,1)S(1)} %get-tuple-element.28.refs_2_, ...), custom_call_target="tpu_custom_call" | custom-call | tf_op jit(solution)/shard_map/backward/pallas_call | solution.py:363
